TPU v7x, 256 devices: a whole 4x4x8 slice. The times are simulated.
256 devices in a mesh: band: 32 (over x_hi, z, core), var: 8 (over y, x_lo).
Axes of the slice: x: 4 (x_hi: 2, x_lo: 2; x = x_hi * 2 + x_lo), y: 4, z: 8, core: 2. Of those that a mesh axis runs over, the one named last changes fastest.
Arguments:
- patches: bfloat16 [16, 32, 256, 64], P('var', 'band'), may hold values from -6 to 6
- w_embed: bfloat16 [16, 64, 2048], P('var'), may hold values from -0.75 to 0.75
- var_bias: float32 [16, 2048], P('var'), may hold values from -3 to 3
- agg_gain: float32 [2048], replicated, may hold values from 0.1 to 1.9
- wq: bfloat16 [2048, 2048], P(None, 'var'), may hold values from -4 to 4
- wk: bfloat16 [2048, 2048], P(None, 'var'), may hold values from -4 to 4
- wv: bfloat16 [2048, 2048], P(None, 'var'), may hold values from -0.125 to 0.125
- wo: bfloat16 [2048, 2048], P('var'), may hold values from -0.125 to 0.125
- w_up: bfloat16 [2048, 1024], replicated, may hold values from -0.125 to 0.125
- conv1: bfloat16 [9, 64, 64], replicated, may hold values from -0.25 to 0.25
- bias1: float32 [64], replicated, may hold values from -3 to 3
- conv2: bfloat16 [9, 64, 64], replicated, may hold values from -0.25 to 0.25
- cotangent: bfloat16 [128, 64, 1024], P('band', None, 'var'), may hold values from -6 to 6
Outputs:
- field_out: bfloat16 [128, 64, 1024], P('band', None, 'var')
- grad_fine: bfloat16 [128, 64, 1024], P('band', None, 'var')
- grad_conv1: float32 [9, 64, 64], replicated
- grad_conv2: float32 [9, 64, 64], replicated
- grad_bias: float32 [64], replicated
All inputs are finite; a program needn't handle non-finite values.
Results may differ from a plain program's by a relative error of at most 0.03.
Values may be sent and summed in bfloat16 or wider, within the bound.
No kernel may reach another device: no remote copies, remote signals or barrier semaphores. Data moves between devices by JAX's collectives and lax.ppermute only.
A program may use at most 128 MiB of HBM per device.

v0:
```python
import math
import jax
import jax.numpy as jnp
from jax import lax
from jax.sharding import PartitionSpec as P

D = 2048
HD = 128
C = 64
R = 4


def with_halo(cells, sides, width):
    for axis, dim in sides:
        count = lax.axis_size(axis)
        ends = count - 1
        head = lax.slice_in_dim(cells, 0, width, axis=dim)
        tail = lax.slice_in_dim(cells, cells.shape[dim] - width, cells.shape[dim], axis=dim)
        cells = jnp.concatenate(
            [
                lax.ppermute(tail, axis, [(i, (i + 1) % count) for i in range(ends)]),
                cells,
                lax.ppermute(head, axis, [((i + 1) % count, i) for i in range(ends)]),
            ],
            axis=dim,
        )
    return cells


def tap_stack(padded, height, width):
    pieces = [
        padded[row_tap : row_tap + height, :, col_tap : col_tap + width]
        for row_tap in range(3)
        for col_tap in range(3)
    ]
    return jnp.concatenate(pieces, axis=1)


def conv_padded(padded, weight, height, width):
    stacked = tap_stack(padded, height, width)
    return jnp.einsum(
        "ykx,ko->yox",
        stacked,
        weight.reshape(-1, weight.shape[2]),
        preferred_element_type=jnp.float32,
    )


def flipped(weight):
    return jnp.transpose(weight[::-1], (0, 2, 1))


def weight_grad(padded, grads):
    stacked = tap_stack(padded, grads.shape[0], grads.shape[2])
    summed = jnp.einsum("ykx,yox->ko", stacked, grads, preferred_element_type=jnp.float32)
    return summed.reshape(9, padded.shape[1], grads.shape[1])


def normalize(mixed, agg_gain):
    return (
        mixed * lax.rsqrt(jnp.mean(mixed * mixed, axis=-1, keepdims=True) + 1e-05) * agg_gain
    ).astype(jnp.bfloat16)


def gradient_rim(field):
    return with_halo(field, (("band", 0), ("var", 2)), 1)


def on_device(
    patches, w_embed, var_bias, agg_gain, wq, wk, wv, wo, w_up, conv1, bias1, conv2, cotangent
):
    var_count = lax.axis_size("var")
    band_count = lax.axis_size("band")
    var_local, lat_dev, lon_all, patch_len = patches.shape
    lon_dev = lon_all // var_count
    flattened = jnp.transpose(patches, (1, 2, 0, 3)).reshape(
        lat_dev * lon_all, var_local * patch_len
    )
    partial_mix = jnp.dot(
        flattened, w_embed.reshape(var_local * patch_len, D), preferred_element_type=jnp.float32
    )
    partial_mix = (partial_mix + jnp.sum(var_bias, axis=0)).reshape(lat_dev, lon_all, D)
    mixed = lax.psum(partial_mix.astype(jnp.bfloat16), "var").astype(jnp.float32)
    normed_band = normalize(mixed, agg_gain)
    normed_slab = lax.dynamic_slice_in_dim(normed_band, lax.axis_index("var") * lon_dev, lon_dev, 1)
    token_rows = jnp.transpose(
        normed_band.reshape(lat_dev, var_count, lon_dev, D), (1, 0, 2, 3)
    ).reshape(-1, D)
    heads_local = wq.shape[1] // HD
    query_rows = token_rows.shape[0]
    queries = jnp.dot(token_rows, wq, preferred_element_type=jnp.float32).astype(jnp.bfloat16)
    keys_local = jnp.dot(token_rows, wk, preferred_element_type=jnp.float32).astype(jnp.bfloat16)
    values_local = jnp.dot(token_rows, wv, preferred_element_type=jnp.float32).astype(jnp.bfloat16)
    query_heads = queries.reshape(query_rows, heads_local, HD)
    running_max = jnp.full((heads_local, query_rows), -1e30, jnp.float32)
    key_heads = lax.all_gather(keys_local, "band", axis=0, tiled=True).reshape(-1, heads_local, HD)
    value_heads = lax.all_gather(values_local, "band", axis=0, tiled=True).reshape(
        -1, heads_local, HD
    )
    scores = jnp.einsum(
        "qhd,khd->hqk", query_heads, key_heads, preferred_element_type=jnp.float32
    ) / math.sqrt(HD)
    new_max = jnp.maximum(running_max, jnp.max(scores, axis=2))
    weights = jnp.exp(scores - new_max[:, :, None])
    new_sum = jnp.sum(weights, axis=2)
    update = jnp.einsum(
        "hqk,khd->hqd",
        weights.astype(jnp.bfloat16),
        value_heads,
        preferred_element_type=jnp.float32,
    )
    context = (update / new_sum[:, :, None]).astype(jnp.bfloat16)
    context = jnp.transpose(context, (1, 0, 2)).reshape(query_rows, heads_local * HD)
    slab_rows = lat_dev * lon_dev
    attended = lax.psum_scatter(
        jnp.dot(context, wo, preferred_element_type=jnp.float32).astype(jnp.bfloat16),
        "var",
        scatter_dimension=0,
        tiled=True,
    ).astype(jnp.float32)
    hidden = (normed_slab.reshape(slab_rows, D).astype(jnp.float32) + attended).astype(jnp.bfloat16)
    upsampled = jnp.dot(hidden, w_up, preferred_element_type=jnp.float32).astype(jnp.bfloat16)
    height = lat_dev * R
    width = lon_dev * R
    upsampled = jnp.transpose(
        upsampled.reshape(lat_dev, lon_dev, R, R, C), (0, 2, 4, 1, 3)
    ).reshape(height, C, width)
    bias_cols = bias1[None, :, None]
    fine_pad = with_halo(upsampled, (("band", 0), ("var", 2)), 1)
    pre = conv_padded(fine_pad, conv1, height, width) + bias_cols
    active = jax.nn.gelu(pre).astype(jnp.bfloat16)
    active_pad = with_halo(active, (("band", 0), ("var", 2)), 1)
    field_out = (
        conv_padded(active_pad, conv2, height, width) + upsampled.astype(jnp.float32)
    ).astype(jnp.bfloat16)
    cotangent_pad = gradient_rim(cotangent)
    d_active = conv_padded(cotangent_pad, flipped(conv2), height, width)
    d_pre = jax.vjp(jax.nn.gelu, pre)[1](d_active)[0].astype(jnp.bfloat16)
    d_pre_pad = gradient_rim(d_pre)
    grad_fine = (
        cotangent.astype(jnp.float32) + conv_padded(d_pre_pad, flipped(conv1), height, width)
    ).astype(jnp.bfloat16)
    factor = 1.0 / math.sqrt(height * band_count * width * var_count)
    first_terms = weight_grad(fine_pad, d_pre) * factor
    second_terms = weight_grad(active_pad, cotangent) * factor
    bias_terms = jnp.sum(d_pre.astype(jnp.float32), axis=(0, 2)) * factor
    grad_conv1, grad_conv2, grad_bias = lax.psum(
        (first_terms, second_terms, bias_terms), ("band", "var")
    )
    return (field_out, grad_fine, grad_conv1, grad_conv2, grad_bias)


def solution(mesh):
    in_specs = (
        P("var", "band", None, None),
        P("var", None, None),
        P("var", None),
        P(),
        P(None, "var"),
        P(None, "var"),
        P(None, "var"),
        P("var", None),
        P(),
        P(),
        P(),
        P(),
        P("band", None, "var"),
    )
    out_specs = (P("band", None, "var"), P("band", None, "var"), P(), P(), P())
    return jax.shard_map(
        on_device, mesh=mesh, in_specs=in_specs, out_specs=out_specs, check_vma=False
    )
```

profile of v0, /device:TPU:1, one launch (start us, length us, event | category | flops | bytes accessed | tf_op | source)
XLA Modules:
  0.0 733.0 jit_solution(12546269796696864949)
XLA Ops:
  7.2 0.9 reduce_sum.36
  8.1 2.5 fusion.10
  10.7 85.5 %all-reduce.4.cloned.1.call-done = bf16[1,256,2048]{2,1,0:T(8,128)(2,1)} async-done(((bf16[1,256,2048]{2,1,0:T(8,128)(2,1)}), bf16[1,256,2048]{2,1,0:T(8,128)(2,1)}) %all-reduce.4.cloned.1.call-update) | async-done | bytes 1048592 | tf_op jit(solution)/shard_map/psum | solution.py:83
  96.2 1.5 fusion.11
  97.7 1.5 fusion.13
  99.3 1.1 convolution_convert_fusion.2
  100.4 2.3 convolution_convert_fusion.1
  102.8 1.7 convolution_convert_fusion.3
  104.6 86.7 %all-gather.3.cloned.1.call-done = bf16[8192,256]{1,0:T(8,128)(2,1)} async-done(((bf16[256,256]{1,0:T(8,128)(2,1)}), bf16[8192,256]{1,0:T(8,128)(2,1)}) %all-gather.3.cloned.1.call-update) | async-done | bytes 4194320 | tf_op jit(solution)/shard_map/all_gather | solution.py:96
  191.3 9.3 %multiply_reduce_fusion = (f32[2,256]{1,0:T(2,128)S(1)}, f32[2,256,8192]{2,1,0:T(8,128)}) fusion(bf16[256,2,128]{0,2,1:T(8,128)(2,1)S(1)} %bitcast.117, bf16[8192,256]{1,0:T(8,128)(2,1)} %all-gather.3.cloned.1.call-done), kind=kOutput, calls=%fused_computation.1 | convolution fusion | flops 1082129920 | bytes 21104640 | tf_op jit(solution)/shard_map/qhd,khd->hqk/dot_general | solution.py:100
  200.6 8.8 %fusion = f32[2,256]{1,0:T(2,128)S(1)} fusion(f32[2,256,8192]{2,1,0:T(8,128)} %get-tuple-element.32, f32[2,256]{1,0:T(2,128)S(1)} %broadcast_maximum_fusion), kind=kLoop, calls=%fused_computation.2 | loop fusion | flops 12582400 | bytes 16781312 | tf_op jit(solution)/shard_map/reduce_sum | solution.py:105
  209.4 68.6 %all-gather.5.cloned.1.call-done = bf16[8192,256]{1,0:T(8,128)(2,1)} async-done(((bf16[256,256]{1,0:T(8,128)(2,1)}), bf16[8192,256]{1,0:T(8,128)(2,1)}) %all-gather.5.cloned.1.call-update) | async-done | bytes 4194320 | tf_op jit(solution)/shard_map/all_gather | solution.py:97
  278.0 6.4 copy.52
  284.4 10.4 %fusion.27 = bf16[256,2,128]{0,2,1:T(8,128)(2,1)S(1)} fusion(bf16[8192,2,128]{0,2,1:T(8,128)(2,1)} %bitcast.110, f32[2,256,8192]{2,1,0:T(8,128)} %get-tuple-element.32, f32[2,256]{1,0:T(2,128)S(1)} %broadcast_maximum_fusion, f32[256,2]{0,1:T(2,128)S(1)} %bitcast.125), kind=kOutput, calls=%fused_computation.38 | convolution fusion | flops 1086455808 | bytes 21106688 | tf_op jit(solution)/shard_map/hqk,khd->hqd/dot_general | solution.py:106
  294.8 1.5 convolution_convert_fusion
  296.4 3.0 collective-permute-start.8
  299.4 1.9 collective-permute-start.9
  301.5 3.0 collective-permute-done.9
  304.6 2.2 collective-permute-start.10
  306.8 0.1 copy.41
  307.0 0.2 copy.43
  307.1 1.5 collective-permute-start.11
  308.6 0.3 collective-permute-done.10
  308.9 0.7 constant_dynamic-update-slice_fusion.29
  309.6 1.4 constant_dynamic-update-slice_fusion.28
  311.0 6.8 collective-permute-done.11
  317.8 0.7 constant_dynamic-update-slice_fusion.27
  318.5 0.7 constant_dynamic-update-slice_fusion.26
  319.2 0.6 constant_dynamic-update-slice_fusion.25
  319.8 0.8 constant_dynamic-update-slice_fusion.24
  320.6 0.7 constant_dynamic-update-slice_fusion.23
  321.3 11.4 %reduce-scatter.2.cloned.1.call-done = bf16[32,2048]{1,0:T(8,128)(2,1)} async-done(((bf16[256,2048]{1,0:T(8,128)(2,1)}), bf16[32,2048]{1,0:T(8,128)(2,1)}) %reduce-scatter.2.cloned.1.call-update) | async-done | bytes 131088 | tf_op jit(solution)/shard_map/reduce_scatter | solution.py:115
  332.7 3.1 convolution_convert_fusion.4
  335.8 0.1 reshape.87
  336.1 8.2 %collective-permute-start = (bf16[1,64,128]{2,1,0:T(8,128)(2,1)S(1)}, bf16[1,64,128]{2,1,0:T(8,128)(2,1)S(1)}, u32[]{:S(2)}, u32[]{:S(2)}) collective-permute-start(bf16[1,64,128]{2,1,0:T(8,128)(2,1)S(1)} %copy.32), channel_id=1, source_target_pairs={{0,8},{8,16},{16,24},{24,32},{32,40},{40,48},{48,56},{56,64},{64,7... | collective-permute-start | bytes 49160 | tf_op jit(solution)/shard_map/ppermute | solution.py:21
  344.4 1.9 collective-permute-start.1
  346.4 0.6 constant_dynamic-update-slice_fusion.22
  347.1 2.4 collective-permute-done.1
  349.6 1.6 collective-permute-start.2
  351.2 1.3 collective-permute-start.3
  352.5 0.7 constant_dynamic-update-slice_fusion.21
  353.2 3.3 collective-permute-done.3
  357.2 0.3 multiply_convert_fusion
  357.5 1.5 convert_reduce_fusion
  359.0 0.3 fusion.17
  359.3 0.9 copy.45
  360.2 3.7 collective-permute-start.4
  363.8 1.9 collective-permute-start.5
  365.8 3.6 collective-permute-start.12
  369.4 1.9 collective-permute-start.13
  371.4 84.9 %psum.31 = f32[64]{0:T(128)} all-reduce(f32[64]{0:T(128)S(1)} %broadcast_multiply_fusion), channel_id=1, replica_groups=mesh['band'=32,'var'=8] {'band','var'}, use_global_device_ids=true, to_apply=%region_9.0 | all-reduce | flops 64 | bytes 512 | tf_op jit(solution)/shard_map/psum | solution.py:147
  456.4 1.3 collective-permute-start.6
  457.7 1.3 collective-permute-start.7
  459.1 4.0 collective-permute-start.14
  463.1 1.3 collective-permute-start.15
  464.4 0.1 pad_maximum_fusion.1
  465.0 0.3 fusion.18
  465.3 0.9 copy.46
  466.2 4.2 collective-permute-done.15
  471.0 0.9 fusion.22
  471.9 0.9 fusion.23
  472.8 250.3 %all-reduce.6.cloned.1.call-done = (f32[9,64,64]{2,1,0:T(8,128)}, f32[9,64,64]{2,1,0:T(8,128)}) async-done(((f32[9,64,64]{2,1,0:T(8,128)}, f32[9,64,64]{2,1,0:T(8,128)}), (f32[9,64,64]{2,1,0:T(8,128)}, f32[9,64,64]{2,1,0:T(8,128)})) %all-reduce.6.cloned.1.call-update) | async-done | bytes 294928 | tf_op jit(solution)/shard_map/psum | solution.py:147
  723.1 1.7 copy.104
  724.7 1.7 copy.105
  (86 shorter events, 2.7 us)
Async XLA Ops:
  7.2 287.6 %copy-start = (bf16[256,2048]{1,0:T(8,128)(2,1)S(1)}, bf16[256,2048]{1,0:T(8,128)(2,1)}, u32[]{:S(2)}) copy-start(bf16[256,2048]{1,0:T(8,128)(2,1)} %param.20) | copy-start | bytes 3145732
  7.2 92.1 %copy-start.2 = (bf16[2048,256]{1,0:T(8,128)(2,1)S(1)}, bf16[2048,256]{1,0:T(8,128)(2,1)}, u32[]{:S(2)}) copy-start(bf16[2048,256]{1,0:T(8,128)(2,1)} %param.18) | copy-start | bytes 3145732
  7.2 89.0 %all-reduce.4.cloned.1.call-start = ((), (), s32[]{:S(2)}) async-start(), calls=%async_computation.1 | async-start | bytes 2097152 | tf_op jit(solution)/shard_map/psum | solution.py:83
  10.6 180.7 %all-gather.3.cloned.1.call-start = ((), (), s32[]{:S(2)}) async-start(), calls=%async_computation.2 | async-start | bytes 4325376 | tf_op jit(solution)/shard_map/all_gather | solution.py:96
  100.4 177.6 %all-gather.5.cloned.1.call-start = ((), (), s32[]{:S(2)}) async-start(), calls=%async_computation.3 | async-start | bytes 4325376 | tf_op jit(solution)/shard_map/all_gather | solution.py:97
  102.8 229.9 %reduce-scatter.2.cloned.1.call-start = ((), (), s32[]{:S(2)}) async-start(), calls=%async_computation.4 | async-start | bytes 1179648 | tf_op jit(solution)/shard_map/reduce_scatter | solution.py:115
  284.4 12.0 %copy-start.1 = (bf16[4,64,128]{2,1,0:T(8,128)(2,1)S(1)}, bf16[4,64,128]{2,1,0:T(8,128)(2,1)}, u32[]{:S(2)}) copy-start(bf16[4,64,128]{2,1,0:T(8,128)(2,1)} %param.25) | copy-start | bytes 196612
  284.4 17.0 %copy-start.3 = (bf16[9,64,64]{2,1,0:T(8,128)(2,1)S(1)}, bf16[9,64,64]{2,1,0:T(8,128)(2,1)}, u32[]{:S(2)}) copy-start(bf16[9,64,64]{2,1,0:T(8,128)(2,1)} %param.24) | copy-start | bytes 221188
  284.4 17.0 %copy-start.4 = (bf16[9,64,64]{2,1,0:T(8,128)(2,1)S(1)}, bf16[9,64,64]{2,1,0:T(8,128)(2,1)}, u32[]{:S(2)}) copy-start(bf16[9,64,64]{2,1,0:T(8,128)(2,1)} %param.22) | copy-start | bytes 221188
  296.3 426.7 %all-reduce.6.cloned.1.call-start = ((), (), s32[]{:S(2)}) async-start(), calls=%async_computation.5 | async-start | bytes 1179648 | tf_op jit(solution)/shard_map/psum | solution.py:147
  296.4 5.0 collective-permute-start.8
  299.4 5.1 collective-permute-start.9
  301.4 3.1 copy-start.5
  304.6 4.3 collective-permute-start.10
  307.1 10.6 %collective-permute-start.11 = (bf16[6,64,1]{2,1,0:T(8,128)(2,1)S(1)}, bf16[6,64,1]{2,1,0:T(8,128)(2,1)S(1)}, u32[]{:S(2)}, u32[]{:S(2)}) collective-permute-start(bf16[6,64,1]{2,1,0:T(8,128)(2,1)S(1)} %get-tuple-element.15), channel_id=1, source_target_pairs={{1,0},{2,1},{3,2},{4,3},{5,4},{6,5},{7,6},{9,8},{10,9},{11,10},{12... | collective-permute-start | bytes 2312 | tf_op jit(solution)/shard_map/ppermute | solution.py:23
  321.3 35.8 %copy-start.6 = (f32[64]{0:T(128)S(1)}, f32[64]{0:T(128)}, u32[]{:S(2)}) copy-start(f32[64]{0:T(128)} %param.23) | copy-start | bytes 772
  336.1 11.0 %collective-permute-start = (bf16[1,64,128]{2,1,0:T(8,128)(2,1)S(1)}, bf16[1,64,128]{2,1,0:T(8,128)(2,1)S(1)}, u32[]{:S(2)}, u32[]{:S(2)}) collective-permute-start(bf16[1,64,128]{2,1,0:T(8,128)(2,1)S(1)} %copy.32), channel_id=1, source_target_pairs={{0,8},{8,16},{16,24},{24,32},{32,40},{40,48},{48,56},{56,64},{64,7... | collective-permute-start | bytes 49160 | tf_op jit(solution)/shard_map/ppermute | solution.py:21
  344.4 5.1 collective-permute-start.1
  349.6 3.6 collective-permute-start.2
  351.2 5.4 collective-permute-start.3
  360.2 96.1 %collective-permute-start.4 = (bf16[1,64,128]{2,1,0:T(8,128)(2,1)S(1)}, bf16[1,64,128]{2,1,0:T(8,128)(2,1)S(1)}, u32[]{:S(2)}, u32[]{:S(2)}) collective-permute-start(bf16[1,64,128]{2,1,0:T(8,128)(2,1)S(1)} %get-tuple-element.29), channel_id=1, source_target_pairs={{0,8},{8,16},{16,24},{24,32},{32,40},{40,48},{48,56},{56,64},{64,7... | collective-permute-start | bytes 49160 | tf_op jit(solution)/shard_map/ppermute | solution.py:21
  363.8 92.4 %collective-permute-start.5 = (bf16[1,64,128]{2,1,0:T(8,128)(2,1)S(1)}, bf16[1,64,128]{2,1,0:T(8,128)(2,1)S(1)}, u32[]{:S(2)}, u32[]{:S(2)}) collective-permute-start(bf16[1,64,128]{2,1,0:T(8,128)(2,1)S(1)} %get-tuple-element.30), channel_id=1, source_target_pairs={{8,0},{16,8},{24,16},{32,24},{40,32},{48,40},{56,48},{64,56},{72,6... | collective-permute-start | bytes 49160 | tf_op jit(solution)/shard_map/ppermute | solution.py:23
  365.8 93.2 %collective-permute-start.12 = (bf16[1,64,128]{2,1,0:T(8,128)(2,1)S(1)}, bf16[1,64,128]{2,1,0:T(8,128)(2,1)S(1)}, u32[]{:S(2)}, u32[]{:S(2)}) collective-permute-start(bf16[1,64,128]{2,1,0:T(8,128)(2,1)S(1)} %get-tuple-element.25), channel_id=1, source_target_pairs={{0,8},{8,16},{16,24},{24,32},{32,40},{40,48},{48,56},{56,64},{64,7... | collective-permute-start | bytes 49160 | tf_op jit(solution)/shard_map/ppermute | solution.py:21
  369.4 89.6 %collective-permute-start.13 = (bf16[1,64,128]{2,1,0:T(8,128)(2,1)S(1)}, bf16[1,64,128]{2,1,0:T(8,128)(2,1)S(1)}, u32[]{:S(2)}, u32[]{:S(2)}) collective-permute-start(bf16[1,64,128]{2,1,0:T(8,128)(2,1)S(1)} %get-tuple-element.26), channel_id=1, source_target_pairs={{8,0},{16,8},{24,16},{32,24},{40,32},{48,40},{56,48},{64,56},{72,6... | collective-permute-start | bytes 49160 | tf_op jit(solution)/shard_map/ppermute | solution.py:23
  456.4 8.1 %collective-permute-start.6 = (bf16[6,64,1]{2,1,0:T(8,128)(2,1)S(1)}, bf16[6,64,1]{2,1,0:T(8,128)(2,1)S(1)}, u32[]{:S(2)}, u32[]{:S(2)}) collective-permute-start(bf16[6,64,1]{2,1,0:T(8,128)(2,1)S(1)} %get-tuple-element.20), channel_id=1, source_target_pairs={{0,1},{1,2},{2,3},{3,4},{4,5},{5,6},{6,7},{8,9},{9,10},{10,11},{11... | collective-permute-start | bytes 2312 | tf_op jit(solution)/shard_map/ppermute | solution.py:21
  457.7 6.8 collective-permute-start.7
  459.1 7.1 collective-permute-start.14
  463.1 7.3 collective-permute-start.15
Sparse Core Ops, SparseCore 0:
  10.8 85.3 all-reduce.3
  100.5 90.7 all-gather.2
  194.7 83.2 all-gather.4
  296.4 36.2 reduce-scatter.1
  472.0 250.9 all-reduce.5
where the time goes:
time: 734 us; the launch traced here: 733 us
  waiting for transfers between devices  523 us (71%)
  blocking collectives  84.9 us (12%)
  starting transfers between devices  40.9 us (6%)
  matrix products  36.1 us (5%)
  other arithmetic  19.6 us (3%)
  local copies, waits for them, and re-layouts  14.5 us (2%)
  between operations  14.4 us (2%)
    psum x1, waiting for transfers between devices, on_device(): lax.psum((first_terms, second_terms, bias_terms), ('band', 'var'))  250 us
    all_gather x1, waiting for transfers between devices, on_device(): lax.all_gather(keys_local, 'band', axis=0, tiled=True)  86.7 us
    psum x1, waiting for transfers between devices, on_device(): lax.psum(partial_mix.astype(jnp.bfloat16), 'var').astype(jnp.float32)  85.5 us
    psum x1, blocking collectives, on_device(): lax.psum((first_terms, second_terms, bias_terms), ('band', 'var'))  84.9 us
    all_gather x1, waiting for transfers between devices, on_device(): lax.all_gather(values_local, 'band', axis=0, tiled=True)  68.6 us
    ppermute x8, starting transfers between devices, with_halo(): lax.ppermute(tail, axis, [(i, (i + 1) % count) for i in range(ends)])  27.6 us
    ppermute x8, waiting for transfers between devices, with_halo(): lax.ppermute(head, axis, [((i + 1) % count, i) for i in range(ends)])  19.7 us
  transfers between devices with their start and end apart: 21, of which 11 were waited for; matrix products, arithmetic and copies ran while one was open for 4% of the time, Pallas kernels for 0%

commit v1 on v0

--- a/solution.py
+++ b/solution.py
@@ -80,7 +80,9 @@
         flattened, w_embed.reshape(var_local * patch_len, D), preferred_element_type=jnp.float32
     )
     partial_mix = (partial_mix + jnp.sum(var_bias, axis=0)).reshape(lat_dev, lon_all, D)
-    mixed = lax.psum(partial_mix.astype(jnp.bfloat16), "var").astype(jnp.float32)
+    mixed = jnp.sum(lax.all_gather(partial_mix.astype(jnp.bfloat16), "var"), axis=0).astype(
+        jnp.float32
+    )
     normed_band = normalize(mixed, agg_gain)
     normed_slab = lax.dynamic_slice_in_dim(normed_band, lax.axis_index("var") * lon_dev, lon_dev, 1)
     token_rows = jnp.transpose(

time: 734 us -> 822 us (1.12)
  waiting for transfers between devices: 523 us -> 607 us
    all_gather x0 -> x1, waiting for transfers between devices: none -> 175 us  [on_device(): lax.all_gather(partial_mix.astype(jnp.bfloat16), 'var')]
    psum x1 -> x0, waiting for transfers between devices: 85.5 us -> none  [on_device(): lax.psum(partial_mix.astype(jnp.bfloat16), 'var').astype(jnp.float32)]
    reduce_scatter x1, waiting for transfers between devices: 11.4 us -> 22.1 us  [on_device(): lax.psum_scatter(jnp.dot(context, wo, preferred_element_type=jnp.float32)...]
    all_gather x1, waiting for transfers between devices: 86.7 us -> 77.8 us  [on_device(): lax.all_gather(keys_local, 'band', axis=0, tiled=True)]
  transfers between devices with their start and end apart: 21 -> 21, of which waited for: 11 -> 10; matrix products, arithmetic and copies ran while one was open for 4% -> 6% of each run, Pallas kernels for 0% -> 0%
where the time goes in v1:
time: 822 us; the launch traced here: 821 us
  waiting for transfers between devices  607 us (74%)
  blocking collectives  84.7 us (10%)
  starting transfers between devices  41.8 us (5%)
  matrix products  36.6 us (4%)
  other arithmetic  20 us (2%)
  local copies, waits for them, and re-layouts  16 us (2%)
  between operations  14.4 us (2%)
    psum x1, waiting for transfers between devices, on_device(): lax.psum((first_terms, second_terms, bias_terms), ('band', 'var'))  250 us
    all_gather x1, waiting for transfers between devices, on_device(): lax.all_gather(partial_mix.astype(jnp.bfloat16), 'var')  175 us
    psum x1, blocking collectives, on_device(): lax.psum((first_terms, second_terms, bias_terms), ('band', 'var'))  84.7 us
    all_gather x1, waiting for transfers between devices, on_device(): lax.all_gather(keys_local, 'band', axis=0, tiled=True)  77.8 us
    all_gather x1, waiting for transfers between devices, on_device(): lax.all_gather(values_local, 'band', axis=0, tiled=True)  68.6 us
    ppermute x8, starting transfers between devices, with_halo(): lax.ppermute(tail, axis, [(i, (i + 1) % count) for i in range(ends)])  28.4 us
    reduce_scatter x1, waiting for transfers between devices, on_device(): lax.psum_scatter(jnp.dot(context, wo, preferred_element_type=jnp.float32)...  22.1 us
  transfers between devices with their start and end apart: 21, of which 10 were waited for; matrix products, arithmetic and copies ran while one was open for 6% of the time, Pallas kernels for 0%

profile of v1, /device:TPU:1, one launch (start us, length us, event | category | flops | bytes accessed | tf_op | source)
XLA Modules:
  0.0 820.9 jit_solution(8939703048559889483)
XLA Ops:
  7.2 0.8 reduce_sum.48
  8.0 2.6 fusion.9
  10.7 174.6 %all-gather.9.cloned.1.call-done = bf16[2048,2048]{1,0:T(8,128)(2,1)} async-done(((bf16[256,2048]{1,0:T(8,128)(2,1)}), bf16[2048,2048]{1,0:T(8,128)(2,1)}) %all-gather.9.cloned.1.call-update) | async-done | bytes 8388624 | tf_op jit(solution)/shard_map/all_gather | solution.py:83
  185.3 5.3 reduce.4
  190.6 0.3 fusion.10
  190.9 1.1 convolution_convert_fusion.2
  192.2 2.4 convolution_convert_fusion.1
  194.6 3.9 collective-permute-start.8
  198.5 2.1 collective-permute-start.9
  200.6 1.9 convolution_convert_fusion.3
  202.6 77.8 %all-gather.5.cloned.1.call-done = bf16[8192,256]{1,0:T(8,128)(2,1)} async-done(((bf16[256,256]{1,0:T(8,128)(2,1)}), bf16[8192,256]{1,0:T(8,128)(2,1)}) %all-gather.5.cloned.1.call-update) | async-done | bytes 4194320 | tf_op jit(solution)/shard_map/all_gather | solution.py:98
  280.4 9.3 %multiply_reduce_fusion = (f32[2,256]{1,0:T(2,128)S(1)}, f32[2,256,8192]{2,1,0:T(8,128)}) fusion(bf16[256,2,128]{0,2,1:T(8,128)(2,1)S(1)} %bitcast.116, bf16[8192,256]{1,0:T(8,128)(2,1)} %all-gather.5.cloned.1.call-done), kind=kOutput, calls=%fused_computation.1 | convolution fusion | flops 1082129920 | bytes 21104640 | tf_op jit(solution)/shard_map/qhd,khd->hqk/dot_general | solution.py:102
  289.7 8.8 %fusion = f32[2,256]{1,0:T(2,128)S(1)} fusion(f32[2,256,8192]{2,1,0:T(8,128)} %get-tuple-element.32, f32[2,256]{1,0:T(2,128)S(1)} %broadcast_maximum_fusion), kind=kLoop, calls=%fused_computation.2 | loop fusion | flops 12582400 | bytes 16781312 | tf_op jit(solution)/shard_map/reduce_sum | solution.py:107
  298.4 68.6 %all-gather.7.cloned.1.call-done = bf16[8192,256]{1,0:T(8,128)(2,1)} async-done(((bf16[256,256]{1,0:T(8,128)(2,1)}), bf16[8192,256]{1,0:T(8,128)(2,1)}) %all-gather.7.cloned.1.call-update) | async-done | bytes 4194320 | tf_op jit(solution)/shard_map/all_gather | solution.py:99
  367.1 6.4 copy.71
  373.5 10.4 %fusion.26 = bf16[256,2,128]{0,2,1:T(8,128)(2,1)S(1)} fusion(bf16[8192,2,128]{0,2,1:T(8,128)(2,1)} %bitcast.104, f32[2,256,8192]{2,1,0:T(8,128)} %get-tuple-element.32, f32[2,256]{1,0:T(2,128)S(1)} %broadcast_maximum_fusion, f32[256,2]{0,1:T(2,128)S(1)} %bitcast.120), kind=kOutput, calls=%fused_computation.38 | convolution fusion | flops 1086455808 | bytes 21106688 | tf_op jit(solution)/shard_map/hqk,khd->hqd/dot_general | solution.py:108
  383.9 1.4 convolution_convert_fusion
  385.7 0.4 copy-done.4
  386.1 2.2 collective-permute-start.10
  388.3 0.1 copy.60
  388.5 0.2 copy.62
  388.6 1.3 collective-permute-start.11
  389.9 0.2 collective-permute-done.10
  390.3 0.7 constant_dynamic-update-slice_fusion.28
  391.0 4.3 collective-permute-done.11
  395.5 0.1 constant_dynamic-update-slice_fusion.24
  395.8 0.8 copy-done.6
  396.6 0.8 dynamic-slice
  397.3 1.6 convert_bitcast_fusion
  398.9 22.1 %reduce-scatter.2.cloned.1.call-done = bf16[32,2048]{1,0:T(8,128)(2,1)} async-done(((bf16[256,2048]{1,0:T(8,128)(2,1)}), bf16[32,2048]{1,0:T(8,128)(2,1)}) %reduce-scatter.2.cloned.1.call-update) | async-done | bytes 131088 | tf_op jit(solution)/shard_map/reduce_scatter | solution.py:117
  421.1 3.2 convolution_convert_fusion.4
  424.3 0.1 reshape.161
  424.6 8.7 %collective-permute-start = (bf16[1,64,128]{2,1,0:T(8,128)(2,1)S(1)}, bf16[1,64,128]{2,1,0:T(8,128)(2,1)S(1)}, u32[]{:S(2)}, u32[]{:S(2)}) collective-permute-start(bf16[1,64,128]{2,1,0:T(8,128)(2,1)S(1)} %copy.51), channel_id=1, source_target_pairs={{0,8},{8,16},{16,24},{24,32},{32,40},{40,48},{48,56},{56,64},{64,7... | collective-permute-start | bytes 49160 | tf_op jit(solution)/shard_map/ppermute | solution.py:21
  433.4 1.9 collective-permute-start.1
  435.4 0.6 constant_dynamic-update-slice_fusion.22
  436.1 2.4 collective-permute-done.1
  438.6 1.3 collective-permute-start.2
  439.9 1.3 collective-permute-start.3
  441.2 0.7 constant_dynamic-update-slice_fusion.21
  442.0 3.3 collective-permute-done.3
  445.3 0.1 pad_maximum_fusion
  445.9 0.3 multiply_convert_fusion
  446.2 1.5 convert_reduce_fusion
  447.7 0.3 fusion.16
  448.0 0.9 copy.64
  448.9 3.6 collective-permute-start.4
  452.5 2.1 collective-permute-start.5
  454.6 3.4 collective-permute-start.12
  458.0 1.9 collective-permute-start.13
  460.0 84.7 %psum.23 = f32[64]{0:T(128)} all-reduce(f32[64]{0:T(128)S(1)} %broadcast_multiply_fusion), channel_id=1, replica_groups=mesh['band'=32,'var'=8] {'band','var'}, use_global_device_ids=true, to_apply=%region_9.0 | all-reduce | flops 64 | bytes 512 | tf_op jit(solution)/shard_map/psum | solution.py:149
  544.8 1.3 collective-permute-start.6
  546.1 1.3 collective-permute-start.7
  547.6 4.0 collective-permute-start.14
  551.6 1.3 collective-permute-start.15
  552.9 0.1 pad_maximum_fusion.1
  553.5 0.3 fusion.17
  553.8 0.9 copy.65
  554.7 3.9 collective-permute-done.15
  558.6 0.1 pad_maximum_fusion.2
  559.1 0.9 fusion.21
  560.1 0.9 fusion.22
  561.0 250.0 %all-reduce.3.cloned.1.call-done = (f32[9,64,64]{2,1,0:T(8,128)}, f32[9,64,64]{2,1,0:T(8,128)}) async-done(((f32[9,64,64]{2,1,0:T(8,128)}, f32[9,64,64]{2,1,0:T(8,128)}), (f32[9,64,64]{2,1,0:T(8,128)}, f32[9,64,64]{2,1,0:T(8,128)})) %all-reduce.3.cloned.1.call-update) | async-done | bytes 294928 | tf_op jit(solution)/shard_map/psum | solution.py:149
  810.9 1.7 copy.122
  812.6 1.7 copy.123
  (94 shorter events, 2.9 us)
Async XLA Ops:
  7.2 376.8 %copy-start = (bf16[256,2048]{1,0:T(8,128)(2,1)S(1)}, bf16[256,2048]{1,0:T(8,128)(2,1)}, u32[]{:S(2)}) copy-start(bf16[256,2048]{1,0:T(8,128)(2,1)} %param.20) | copy-start | bytes 3145732
  7.2 178.1 %all-gather.9.cloned.1.call-start = ((), (), s32[]{:S(2)}) async-start(), calls=%async_computation.4 | async-start | bytes 9437184 | tf_op jit(solution)/shard_map/all_gather | solution.py:83
  10.7 269.7 %all-gather.5.cloned.1.call-start = ((), (), s32[]{:S(2)}) async-start(), calls=%async_computation.1 | async-start | bytes 4325376 | tf_op jit(solution)/shard_map/all_gather | solution.py:98
  185.3 5.6 copy-start.5
  185.3 5.6 copy-start.8
  190.6 4.0 copy-start.1
  190.9 11.6 %copy-start.7 = (f32[256]{0:T(256)}, f32[256]{0:T(256)S(1)}, u32[]{:S(2)}) copy-start(f32[256]{0:T(256)S(1)} %add_rsqrt_fusion) | copy-start | bytes 3076
  192.1 175.0 %all-gather.7.cloned.1.call-start = ((), (), s32[]{:S(2)}) async-start(), calls=%async_computation.2 | async-start | bytes 4325376 | tf_op jit(solution)/shard_map/all_gather | solution.py:99
  194.6 226.5 %reduce-scatter.2.cloned.1.call-start = ((), (), s32[]{:S(2)}) async-start(), calls=%async_computation.3 | async-start | bytes 1179648 | tf_op jit(solution)/shard_map/reduce_scatter | solution.py:117
  194.6 190.9 %collective-permute-start.8 = (bf16[1,64,128]{2,1,0:T(8,128)(2,1)S(1)}, bf16[1,64,128]{2,1,0:T(8,128)(2,1)S(1)}, u32[]{:S(2)}, u32[]{:S(2)}) collective-permute-start(bf16[1,64,128]{2,1,0:T(8,128)(2,1)S(1)} %get-tuple-element.28), channel_id=1, source_target_pairs={{0,8},{8,16},{16,24},{24,32},{32,40},{40,48},{48,56},{56,64},{64,7... | collective-permute-start | bytes 49160 | tf_op jit(solution)/shard_map/ppermute | solution.py:21
  198.5 187.0 %collective-permute-start.9 = (bf16[1,64,128]{2,1,0:T(8,128)(2,1)S(1)}, bf16[1,64,128]{2,1,0:T(8,128)(2,1)S(1)}, u32[]{:S(2)}, u32[]{:S(2)}) collective-permute-start(bf16[1,64,128]{2,1,0:T(8,128)(2,1)S(1)} %get-tuple-element.27), channel_id=1, source_target_pairs={{8,0},{16,8},{24,16},{32,24},{40,32},{48,40},{56,48},{64,56},{72,6... | collective-permute-start | bytes 49160 | tf_op jit(solution)/shard_map/ppermute | solution.py:23
  373.5 12.0 %copy-start.2 = (bf16[9,64,64]{2,1,0:T(8,128)(2,1)S(1)}, bf16[9,64,64]{2,1,0:T(8,128)(2,1)}, u32[]{:S(2)}) copy-start(bf16[9,64,64]{2,1,0:T(8,128)(2,1)} %param.24) | copy-start | bytes 221188
  373.5 12.0 %copy-start.3 = (bf16[9,64,64]{2,1,0:T(8,128)(2,1)S(1)}, bf16[9,64,64]{2,1,0:T(8,128)(2,1)}, u32[]{:S(2)}) copy-start(bf16[9,64,64]{2,1,0:T(8,128)(2,1)} %param.22) | copy-start | bytes 221188
  385.4 425.5 %all-reduce.3.cloned.1.call-start = ((), (), s32[]{:S(2)}) async-start(), calls=%async_computation.5 | async-start | bytes 1179648 | tf_op jit(solution)/shard_map/psum | solution.py:149
  385.5 0.6 copy-start.4
  386.1 4.0 collective-permute-start.10
  388.6 6.7 collective-permute-start.11
  395.8 0.8 copy-start.6
  398.9 46.9 %copy-start.9 = (f32[64]{0:T(128)S(1)}, f32[64]{0:T(128)}, u32[]{:S(2)}) copy-start(f32[64]{0:T(128)} %param.23) | copy-start | bytes 772
  424.6 11.5 %collective-permute-start = (bf16[1,64,128]{2,1,0:T(8,128)(2,1)S(1)}, bf16[1,64,128]{2,1,0:T(8,128)(2,1)S(1)}, u32[]{:S(2)}, u32[]{:S(2)}) collective-permute-start(bf16[1,64,128]{2,1,0:T(8,128)(2,1)S(1)} %copy.51), channel_id=1, source_target_pairs={{0,8},{8,16},{16,24},{24,32},{32,40},{40,48},{48,56},{56,64},{64,7... | collective-permute-start | bytes 49160 | tf_op jit(solution)/shard_map/ppermute | solution.py:21
  433.4 5.1 collective-permute-start.1
  438.6 3.3 collective-permute-start.2
  439.9 5.4 collective-permute-start.3
  448.9 95.8 %collective-permute-start.4 = (bf16[1,64,128]{2,1,0:T(8,128)(2,1)S(1)}, bf16[1,64,128]{2,1,0:T(8,128)(2,1)S(1)}, u32[]{:S(2)}, u32[]{:S(2)}) collective-permute-start(bf16[1,64,128]{2,1,0:T(8,128)(2,1)S(1)} %get-tuple-element.29), channel_id=1, source_target_pairs={{0,8},{8,16},{16,24},{24,32},{32,40},{40,48},{48,56},{56,64},{64,7... | collective-permute-start | bytes 49160 | tf_op jit(solution)/shard_map/ppermute | solution.py:21
  452.5 92.3 %collective-permute-start.5 = (bf16[1,64,128]{2,1,0:T(8,128)(2,1)S(1)}, bf16[1,64,128]{2,1,0:T(8,128)(2,1)S(1)}, u32[]{:S(2)}, u32[]{:S(2)}) collective-permute-start(bf16[1,64,128]{2,1,0:T(8,128)(2,1)S(1)} %get-tuple-element.30), channel_id=1, source_target_pairs={{8,0},{16,8},{24,16},{32,24},{40,32},{48,40},{56,48},{64,56},{72,6... | collective-permute-start | bytes 49160 | tf_op jit(solution)/shard_map/ppermute | solution.py:23
  454.6 92.8 %collective-permute-start.12 = (bf16[1,64,128]{2,1,0:T(8,128)(2,1)S(1)}, bf16[1,64,128]{2,1,0:T(8,128)(2,1)S(1)}, u32[]{:S(2)}, u32[]{:S(2)}) collective-permute-start(bf16[1,64,128]{2,1,0:T(8,128)(2,1)S(1)} %get-tuple-element.25), channel_id=1, source_target_pairs={{0,8},{8,16},{16,24},{24,32},{32,40},{40,48},{48,56},{56,64},{64,7... | collective-permute-start | bytes 49160 | tf_op jit(solution)/shard_map/ppermute | solution.py:21
  458.0 89.4 %collective-permute-start.13 = (bf16[1,64,128]{2,1,0:T(8,128)(2,1)S(1)}, bf16[1,64,128]{2,1,0:T(8,128)(2,1)S(1)}, u32[]{:S(2)}, u32[]{:S(2)}) collective-permute-start(bf16[1,64,128]{2,1,0:T(8,128)(2,1)S(1)} %get-tuple-element.26), channel_id=1, source_target_pairs={{8,0},{16,8},{24,16},{32,24},{40,32},{48,40},{56,48},{64,56},{72,6... | collective-permute-start | bytes 49160 | tf_op jit(solution)/shard_map/ppermute | solution.py:23
  544.8 8.1 collective-permute-start.6
  546.1 6.8 collective-permute-start.7
  547.6 7.1 collective-permute-start.14
  551.6 7.0 collective-permute-start.15
Sparse Core Ops, SparseCore 0:
  10.8 174.4 all-gather.8
  192.2 88.1 all-gather.4
  283.7 83.2 all-gather.6
  385.5 35.4 reduce-scatter.1
  560.2 250.7 all-reduce.2
